TPU v7x, 32 devices: a whole 2x2x4 slice. The times are simulated.
32 devices in a mesh: row: 8 (over y, x, core), col: 4 (over z).
Axes of the slice: x: 2, y: 2, z: 4, core: 2. Of those that a mesh axis runs over, the one named last changes fastest.
Arguments:
- matrix: bfloat16 [3072, 3072], P('row', 'col'), may hold values from 3.2484531e-06 to 0.0012969971
- occ_matrix: int32 [24, 24], P('row', 'col'), may hold values 0 or 1
- batch: bfloat16 [3072, 512], P('row', 'col'), may hold values from 0.0099487305 to 4
- occ_batch: int32 [24, 4], P('row', 'col'), may hold values 0 or 1
- prune_mask: int32 [3072, 512], P('row', 'col'), may hold values 0 or 1
Outputs:
- clustered: float32 [3072, 512], P('row', 'col')
All inputs are finite; a program needn't handle non-finite values. No bound on the sum of `occ_matrix` or of `occ_batch` or of `prune_mask` on one device may be relied on, other than what follows from the above.
Results may differ from a plain program's by a relative error of at most 0.0003.
Values may be sent and summed in bfloat16 or wider, within the bound.
A program may use at most 64 MiB of HBM per device.

v0:
```python
import jax
import jax.numpy as jnp
from jax import lax
from jax.sharding import PartitionSpec as P


def expand_tiles(occupancy, size):
    return jnp.repeat(jnp.repeat(occupancy, size, axis=0), size, axis=1)


def body(matrix, occ_matrix, batch, occ_batch, prune_mask):
    tile_size = matrix.shape[0] // occ_matrix.shape[0]
    stored_matrix = matrix * expand_tiles(occ_matrix, tile_size).astype(jnp.bfloat16)
    stored_batch = batch * expand_tiles(occ_batch, tile_size).astype(jnp.bfloat16)
    whole_batch = lax.all_gather(stored_batch, "row", axis=0, tiled=True)
    expanded = jnp.dot(
        lax.all_gather(stored_matrix, "col", axis=1, tiled=True),
        whole_batch,
        preferred_element_type=jnp.float32,
    )
    kept = expanded * prune_mask.astype(jnp.float32)
    inflated = kept * kept
    col_total = lax.psum(jnp.sum(inflated, axis=0), "row")
    order = matrix.shape[0] * lax.axis_size("row")
    return inflated / (col_total[None, :] / order + 1e-05)


def solution(mesh):
    placed = (P("row", "col"), P("row", "col"), P("row", "col"), P("row", "col"), P("row", "col"))
    return jax.shard_map(
        body, mesh=mesh, in_specs=placed, out_specs=P("row", "col"), check_vma=False
    )
```

profile of v0, /device:TPU:0, one launch (start us, length us, event | category | flops | bytes accessed | tf_op | source)
XLA Modules:
  0.0 86.1 jit_solution(16578038678067250543)
XLA Ops:
  6.5 0.0 copy-start.2
  6.5 0.0 copy-start.1
  6.5 0.0 copy-start
  6.5 0.0 all-gather.2.cloned.1.call-start
  6.5 0.7 convert_element_type.25
  7.3 0.1 copy.6
  7.4 0.1 broadcast_bitcast_fusion
  7.5 1.4 %copy.7 = bf16[384,768]{0,1:T(8,128)(2,1)S(1)} copy(bf16[384,768]{1,0:T(8,128)(2,1)} %param.5) | data formatting | bytes 1179648 | tf_op args[0]
  8.8 0.9 %bitcast_multiply_fusion = bf16[384,768]{0,1:T(8,128)(2,1)} fusion(bf16[384,768]{0,1:T(8,128)(2,1)S(1)} %copy.7, bf16[384,6]{0,1:T(8,128)(2,1)S(1)} %bitcast.15), kind=kLoop, calls=%fused_computation.2 | loop fusion | flops 294912 | bytes 1184256 | tf_op jit(solution)/shard_map/mul | solution.py:13
  9.7 0.0 all-gather.2.cloned.1.call-update
  9.7 0.0 copy-done.2
  9.8 0.1 broadcast_bitcast_fusion.1
  9.8 0.0 copy-done.1
  9.8 0.1 broadcast_multiply_fusion
  10.0 11.9 %all_gather.7 = bf16[3072,128]{1,0:T(8,128)(2,1)S(1)} all-gather(bf16[384,128]{1,0:T(8,128)(2,1)S(1)} %broadcast_multiply_fusion), channel_id=1, replica_groups=mesh['row'=8,'col'=4] {'row'}, dimensions={0}, use_global_device_ids=true | all-gather | bytes 884736 | tf_op jit(solution)/shard_map/all_gather | solution.py:15
  21.8 40.8 %all-gather.2.cloned.1.call-done = bf16[384,3072]{0,1:T(8,128)(2,1)} async-done(((bf16[384,768]{0,1:T(8,128)(2,1)}), bf16[384,3072]{0,1:T(8,128)(2,1)}) %all-gather.2.cloned.1.call-update) | async-done | bytes 2359312 | tf_op jit(solution)/shard_map/all_gather | solution.py:17
  62.6 0.0 copy-done
  62.6 2.5 %fusion.1 = (f32[128]{0:T(128)S(1)}, f32[384,128]{1,0:T(8,128)S(1)}) fusion(s32[384,128]{1,0:T(8,128)S(1)} %copy-done, bf16[384,3072]{0,1:T(8,128)(2,1)} %all-gather.2.cloned.1.call-done, bf16[3072,128]{1,0:T(8,128)(2,1)S(1)} %all_gather.7), kind=kOutput, calls=%fused_computation.10 | convolution fusion | flops 302186368 | bytes 3539456 | tf_op jit(solution)/shard_map/dot_general | solution.py:16
  65.1 13.4 %psum.7 = f32[128]{0:T(128)S(1)} all-reduce(f32[128]{0:T(128)S(1)} %get-tuple-element.5), channel_id=1, replica_groups=mesh['row'=8,'col'=4] {'row'}, use_global_device_ids=true, to_apply=%region_1.0 | all-reduce | flops 128 | bytes 1024 | tf_op jit(solution)/shard_map/psum | solution.py:23
  78.5 0.7 broadcast_divide_fusion
  (3 shorter events, 0.0 us)
Async XLA Ops:
  6.5 3.2 %copy-start.2 = (s32[3,1]{0,1:T(1,128)S(1)}, s32[3,1]{0,1:T(1,128)}, u32[]{:S(2)}) copy-start(s32[3,1]{0,1:T(1,128)} %param.8) | copy-start | bytes 40
  6.5 3.3 %copy-start.1 = (bf16[384,128]{1,0:T(8,128)(2,1)S(1)}, bf16[384,128]{1,0:T(8,128)(2,1)}, u32[]{:S(2)}) copy-start(bf16[384,128]{1,0:T(8,128)(2,1)} %param.7) | copy-start | bytes 294916
  6.5 56.1 %copy-start = (s32[384,128]{1,0:T(8,128)S(1)}, s32[384,128]{1,0:T(8,128)}, u32[]{:S(2)}) copy-start(s32[384,128]{1,0:T(8,128)} %param.9) | copy-start | bytes 589828
  6.5 56.1 %all-gather.2.cloned.1.call-start = ((), (), s32[]{:S(2)}) async-start(), calls=%async_computation | async-start | bytes 2949120 | tf_op jit(solution)/shard_map/all_gather | solution.py:17
Sparse Core Ops, SparseCore 0:
  9.9 52.6 all-gather.1
where the time goes:
time: 86.3 us; the launch traced here: 86.1 us
  waiting for transfers between devices  40.8 us (47%)
  blocking collectives  25.3 us (29%)
  between operations  13.4 us (16%)
  matrix products  2.49 us (3%)
  other arithmetic  2.44 us (3%)
  local copies, waits for them, and re-layouts  1.64 us (2%)
    all_gather x1, waiting for transfers between devices, body(): lax.all_gather(stored_matrix, 'col', axis=1, tiled=True)  40.8 us
    psum x1, blocking collectives, body(): col_total = lax.psum(jnp.sum(inflated, axis=0), 'row')  13.4 us
    all_gather x1, blocking collectives, body(): whole_batch = lax.all_gather(stored_batch, 'row', axis=0, tiled=True)  11.9 us
    dot_general x1, matrix products, body(): jnp.dot(lax.all_gather(stored_matrix, 'col', axis=1, tiled=True), whole_b...  2.49 us
  transfers between devices with their start and end apart: 1, of which 1 were waited for; matrix products, arithmetic and copies ran while one was open for 0% of the time, Pallas kernels for 0%

commit v1 on v0

--- a/solution.py
+++ b/solution.py
@@ -2,6 +2,12 @@
 import jax.numpy as jnp
 from jax import lax
 from jax.sharding import PartitionSpec as P
+
+
+def add_all(x, name):
+    shards = lax.all_gather(x, name, axis=0, tiled=False)
+    total = shards.sum(axis=0)
+    return total
 
 
 def expand_tiles(occupancy, size):
@@ -20,7 +26,7 @@
     )
     kept = expanded * prune_mask.astype(jnp.float32)
     inflated = kept * kept
-    col_total = lax.psum(jnp.sum(inflated, axis=0), "row")
+    col_total = add_all(jnp.sum(inflated, axis=0), "row")
     order = matrix.shape[0] * lax.axis_size("row")
     return inflated / (col_total[None, :] / order + 1e-05)
 

time: 86.3 us -> 81.6 us (0.946)
  blocking collectives: 25.3 us -> 20.6 us
    psum x1 -> x0, blocking collectives: 13.4 us -> none  [body(): col_total = lax.psum(jnp.sum(inflated, axis=0), 'row')]
    all_gather x0 -> x1, blocking collectives: none -> 8.75 us  [add_all(): shards = lax.all_gather(x, name, axis=0, tiled=False)]
where the time goes in v1:
time: 81.6 us; the launch traced here: 81.4 us
  waiting for transfers between devices  40.8 us (50%)
  blocking collectives  20.6 us (25%)
  between operations  13.4 us (16%)
  matrix products  2.49 us (3%)
  other arithmetic  2.46 us (3%)
  local copies, waits for them, and re-layouts  1.64 us (2%)
    all_gather x1, waiting for transfers between devices, body(): lax.all_gather(stored_matrix, 'col', axis=1, tiled=True)  40.8 us
    all_gather x1, blocking collectives, body(): whole_batch = lax.all_gather(stored_batch, 'row', axis=0, tiled=True)  11.9 us
    all_gather x1, blocking collectives, add_all(): shards = lax.all_gather(x, name, axis=0, tiled=False)  8.75 us
    dot_general x1, matrix products, body(): jnp.dot(lax.all_gather(stored_matrix, 'col', axis=1, tiled=True), whole_b...  2.49 us
  transfers between devices with their start and end apart: 1, of which 1 were waited for; matrix products, arithmetic and copies ran while one was open for 0% of the time, Pallas kernels for 0%

profile of v1, /device:TPU:0, one launch (start us, length us, event | category | flops | bytes accessed | tf_op | source)
XLA Modules:
  0.0 81.4 jit_solution(8353306862367518985)
XLA Ops:
  6.5 0.0 copy-start.2
  6.5 0.0 copy-start.1
  6.5 0.0 copy-start
  6.5 0.0 all-gather.4.cloned.1.call-start
  6.5 0.7 convert_element_type.25
  7.3 0.1 copy.8
  7.4 0.1 broadcast_bitcast_fusion
  7.5 1.4 %copy.9 = bf16[384,768]{0,1:T(8,128)(2,1)S(1)} copy(bf16[384,768]{1,0:T(8,128)(2,1)} %param.5) | data formatting | bytes 1179648 | tf_op args[0]
  8.8 0.9 %bitcast_multiply_fusion = bf16[384,768]{0,1:T(8,128)(2,1)} fusion(bf16[384,768]{0,1:T(8,128)(2,1)S(1)} %copy.9, bf16[384,6]{0,1:T(8,128)(2,1)S(1)} %bitcast.16), kind=kLoop, calls=%fused_computation.2 | loop fusion | flops 294912 | bytes 1184256 | tf_op jit(solution)/shard_map/mul | solution.py:19
  9.7 0.0 all-gather.4.cloned.1.call-update
  9.7 0.0 copy-done.2
  9.8 0.1 broadcast_bitcast_fusion.1
  9.8 0.0 copy-done.1
  9.8 0.1 broadcast_multiply_fusion
  10.0 11.9 %all_gather.13 = bf16[3072,128]{1,0:T(8,128)(2,1)S(1)} all-gather(bf16[384,128]{1,0:T(8,128)(2,1)S(1)} %broadcast_multiply_fusion), channel_id=1, replica_groups=mesh['row'=8,'col'=4] {'row'}, dimensions={0}, use_global_device_ids=true | all-gather | bytes 884736 | tf_op jit(solution)/shard_map/all_gather | solution.py:21
  21.8 40.8 %all-gather.4.cloned.1.call-done = bf16[384,3072]{0,1:T(8,128)(2,1)} async-done(((bf16[384,768]{0,1:T(8,128)(2,1)}), bf16[384,3072]{0,1:T(8,128)(2,1)}) %all-gather.4.cloned.1.call-update) | async-done | bytes 2359312 | tf_op jit(solution)/shard_map/all_gather | solution.py:23
  62.6 0.0 copy-done
  62.6 2.5 %fusion.1 = (f32[128]{0:T(128)S(1)}, f32[384,128]{1,0:T(8,128)S(1)}) fusion(s32[384,128]{1,0:T(8,128)S(1)} %copy-done, bf16[384,3072]{0,1:T(8,128)(2,1)} %all-gather.4.cloned.1.call-done, bf16[3072,128]{1,0:T(8,128)(2,1)S(1)} %all_gather.13), kind=kOutput, calls=%fused_computation.10 | convolution fusion | flops 302186368 | bytes 3539456 | tf_op jit(solution)/shard_map/dot_general | solution.py:22
  65.1 8.8 %all-gather.1 = f32[8,1,128]{2,1,0:T(1,128)S(1)} all-gather(f32[1,1,128]{2,1,0:T(1,128)S(1)} %bitcast.17), channel_id=2, replica_groups=mesh['row'=8,'col'=4] {'row'}, dimensions={0}, use_global_device_ids=true | all-gather | bytes 4608 | tf_op jit(solution)/shard_map/all_gather | solution.py:8
  73.9 0.7 broadcast_divide_fusion
  (4 shorter events, 0.0 us)
Async XLA Ops:
  6.5 3.2 %copy-start.2 = (s32[3,1]{0,1:T(1,128)S(1)}, s32[3,1]{0,1:T(1,128)}, u32[]{:S(2)}) copy-start(s32[3,1]{0,1:T(1,128)} %param.8) | copy-start | bytes 40
  6.5 3.3 %copy-start.1 = (bf16[384,128]{1,0:T(8,128)(2,1)S(1)}, bf16[384,128]{1,0:T(8,128)(2,1)}, u32[]{:S(2)}) copy-start(bf16[384,128]{1,0:T(8,128)(2,1)} %param.7) | copy-start | bytes 294916
  6.5 56.1 %copy-start = (s32[384,128]{1,0:T(8,128)S(1)}, s32[384,128]{1,0:T(8,128)}, u32[]{:S(2)}) copy-start(s32[384,128]{1,0:T(8,128)} %param.9) | copy-start | bytes 589828
  6.5 56.1 %all-gather.4.cloned.1.call-start = ((), (), s32[]{:S(2)}) async-start(), calls=%async_computation | async-start | bytes 2949120 | tf_op jit(solution)/shard_map/all_gather | solution.py:23
Sparse Core Ops, SparseCore 0:
  9.9 52.6 all-gather.3
